TPU v7x, 128 devices: a whole 4x4x4 slice. The times are simulated.
128 devices in a mesh: leaf: 16 (over z, y), front: 8 (over x, core).
Axes of the slice: x: 4, y: 4, z: 4, core: 2. Of those that a mesh axis runs over, the one named last changes fastest.
Arguments:
- right_side: bfloat16 [32, 81920], P(None, ('leaf', 'front')), may hold values from -6 to 6
- send_order: int32 [81920], P(('leaf', 'front')), may hold values from 0 to 639, as said below
- owner_order: int32 [81920], P(('leaf', 'front')), may hold values from 0 to 639, as said below
- live_rows: int32 [14], replicated, may hold values from 2048 to 4096, as said below
- lower_leaf: bfloat16 [1536, 24576], P(None, ('leaf', 'front')), may hold values from -0.109375 to 0.109375
- upper_leaf: bfloat16 [1536, 24576], P(None, ('leaf', 'front')), may hold values from -0.109375 to 0.109375
- lower_first: bfloat16 [4096, 32768], P(None, ('leaf', 'front')), may hold values from -0.0625 to 0.0625
- lower_second: bfloat16 [4096, 16384], P(None, ('leaf', 'front')), may hold values from -0.0625 to 0.0625
- lower_third: bfloat16 [4096, 8192], P(None, ('leaf', 'front')), may hold values from -0.0625 to 0.0625
- upper_first: bfloat16 [4096, 32768], P(None, ('leaf', 'front')), may hold values from -0.0625 to 0.0625
- upper_second: bfloat16 [4096, 16384], P(None, ('leaf', 'front')), may hold values from -0.0625 to 0.0625
- upper_third: bfloat16 [4096, 8192], P(None, ('leaf', 'front')), may hold values from -0.0625 to 0.0625
- downlink_first: bfloat16 [4096, 24576], P(None, ('leaf', 'front')), may hold values from -0.4375 to 0.4375
- downlink_second: bfloat16 [4096, 32768], P(None, ('leaf', 'front')), may hold values from -0.25 to 0.25
- downlink_third: bfloat16 [4096, 16384], P(None, ('leaf', 'front')), may hold values from -0.25 to 0.25
- uplink_first: bfloat16 [4096, 24576], P(None, ('leaf', 'front')), may hold values from -0.0625 to 0.0625
- uplink_second: bfloat16 [4096, 32768], P(None, ('leaf', 'front')), may hold values from -0.0625 to 0.0625
- uplink_third: bfloat16 [4096, 16384], P(None, ('leaf', 'front')), may hold values from -0.0625 to 0.0625
- pattern_first: int32 [64, 384], P(None, ('leaf', 'front')), may hold values 0 or 1
- pattern_second: int32 [64, 512], P(None, ('leaf', 'front')), may hold values 0 or 1
- pattern_third: int32 [64, 256], P(None, ('leaf', 'front')), may hold values 0 or 1
Outputs:
- solution: bfloat16 [32, 81920], P(None, ('leaf', 'front'))
Inputs may be any that keep to these rules, and one draw needn't show every extreme that they name: `send_order`: each device's 640 entries are a permutation of 0 to 639. `owner_order`: each device's 640 entries are a permutation of 0 to 639. `live_rows`: multiples of 64.
All inputs are finite; a program needn't handle non-finite values. No bound on the sum of `pattern_first` or of `pattern_second` or of `pattern_third` on one device may be relied on, other than what follows from the above.
Results may differ from a plain program's by a relative error of at most 0.023.
Values may be sent and summed in bfloat16 or wider, within the bound.
No kernel may reach another device: no remote copies, remote signals or barrier semaphores. Data moves between devices by JAX's collectives and lax.ppermute only.
A program may use at most 128 MiB of HBM per device.

v0:
```python
import jax
import jax.numpy as jnp
from jax import lax
from jax.sharding import PartitionSpec as P


def partner_2(value, axis, distance):
    mask = 2**distance
    pairs = [(source, source ^ mask) for source in range(lax.axis_size(axis))]
    return lax.ppermute(value, axis, pairs)


def spread(pattern, block):
    wide = jnp.repeat(pattern, block, axis=0)
    return jnp.repeat(wide, block, axis=1).astype(jnp.bfloat16)


def collect_group(portion, level, place):
    gathered = lax.all_gather(portion, "front", axis=1, tiled=True)
    for level_bit in range(level):
        partner = partner_2(gathered, "leaf", level_bit)
        upper_side = place >> level_bit & 1 == 1
        gathered = jnp.where(
            upper_side,
            jnp.concatenate([partner, gathered], axis=1),
            jnp.concatenate([gathered, partner], axis=1),
        )
    return gathered


def leaf_term(portion, matrix):
    return jnp.dot(portion, matrix, preferred_element_type=jnp.float32)


def per_device(
    right_side,
    send_order,
    owner_order,
    live_rows,
    lower_leaf,
    upper_leaf,
    lower_first,
    lower_second,
    lower_third,
    upper_first,
    upper_second,
    upper_third,
    downlink_first,
    downlink_second,
    downlink_third,
    uplink_first,
    uplink_second,
    uplink_third,
    pattern_first,
    pattern_second,
    pattern_third,
):
    fronts = lax.axis_size("front")
    leaves = lax.axis_size("leaf")
    place = lax.axis_index("leaf")
    column = lax.axis_index("front")
    columns = right_side.shape[0]
    leaf_rows = lower_leaf.shape[1]
    sep = lower_first.shape[0]
    lowers = [lower_first, lower_second, lower_third]
    uppers = [upper_first, upper_second, upper_third]
    downs = [downlink_first, downlink_second, downlink_third]
    backs = [uplink_first, uplink_second, uplink_third]
    patterns = [pattern_first, pattern_second, pattern_third]
    block = downlink_first.shape[0] // pattern_first.shape[0]
    pieces = [lower_first.shape[1], lower_second.shape[1], lower_third.shape[1]]
    starts = [0, leaves // 2, leaves // 2 + leaves // 4]
    outgoing = jnp.take(right_side, send_order, axis=1)
    arrived = lax.all_to_all(outgoing, ("leaf", "front"), split_axis=1, concat_axis=1, tiled=True)
    ordered = jnp.take(arrived, owner_order, axis=1)
    leaf_rhs = ordered[:, :leaf_rows]
    level_rhs = []
    offset = leaf_rows
    for level in range(1, 4):
        level_rhs.append(ordered[:, offset : offset + pieces[level - 1]])
        offset = offset + pieces[level - 1]
    piece_masks = []
    full_masks = []
    within = []
    for level in range(1, 4):
        group = 2**level
        member = place & group - 1
        node_live = lax.dynamic_index_in_dim(
            live_rows, starts[level - 1] + (place >> level), 0, keepdims=False
        )
        first_row = (member * fronts + column) * pieces[level - 1]
        piece_masks.append(
            (first_row + jnp.arange(pieces[level - 1], dtype=jnp.int32) < node_live).astype(
                jnp.float32
            )[None, :]
        )
        full_masks.append(
            (jnp.arange(sep, dtype=jnp.int32) < node_live).astype(jnp.float32)[None, :]
        )
        within.append(member)
    expanded = [spread(patterns[index], block) for index in range(3)]
    leaf_y = leaf_term(
        lax.all_gather(leaf_rhs, "front", axis=1, tiled=True), matrix=lower_leaf
    ).astype(jnp.bfloat16)
    children = leaf_y
    level_y = []
    for level in range(1, 4):
        group = 2**level
        piece = pieces[level - 1]
        member = within[level - 1]
        link = downs[level - 1] * expanded[level - 1]
        own_rhs = level_rhs[level - 1].astype(jnp.float32)
        shaped = link.reshape(group, fronts, piece, link.shape[1])
        term = jnp.einsum(
            "kc,jfpc->kfjp", children, shaped, preferred_element_type=jnp.float32
        ).reshape(columns, sep)
        first_row = (column * group + member) * piece
        current = lax.dynamic_slice_in_dim(term, first_row, piece, 1)
        term = lax.dynamic_update_slice_in_dim(term, current - own_rhs, first_row, 1)
        share = lax.psum_scatter(
            term.astype(jnp.bfloat16), "front", scatter_dimension=1, tiled=True
        ).astype(jnp.float32)
        for level_bit in reversed(range(level)):
            middle = share.shape[1] // 2
            lower_half = share[:, :middle]
            upper_half = share[:, middle:]
            high_side = place >> level_bit & 1 == 1
            keeping = jnp.where(high_side, upper_half, lower_half)
            sending = jnp.where(high_side, lower_half, upper_half)
            share = keeping + partner_2(sending.astype(jnp.bfloat16), "leaf", level_bit).astype(
                sending.dtype
            )
        reduced_piece = (-share * piece_masks[level - 1]).astype(jnp.bfloat16)
        reduced_full = collect_group(reduced_piece, level, place)
        solved = jnp.dot(reduced_full, lowers[level - 1], preferred_element_type=jnp.float32)
        found = (solved * piece_masks[level - 1]).astype(jnp.bfloat16)
        level_y.append(found)
        children = found
    level_x = [None, None, None]
    top_full = collect_group(level_y[2], 3, place)
    level_x[2] = (
        jnp.dot(top_full, upper_third, preferred_element_type=jnp.float32) * piece_masks[2]
    ).astype(jnp.bfloat16)
    for level in (2, 1):
        back = backs[level] * expanded[level]
        parent_full = collect_group(level_x[level], level + 1, place)
        update = level_y[level - 1].astype(jnp.float32) - jnp.dot(
            parent_full, back, preferred_element_type=jnp.float32
        )
        reduced = (update * piece_masks[level - 1]).astype(jnp.bfloat16)
        reduced_full = collect_group(reduced, level, place)
        solved = jnp.dot(reduced_full, uppers[level - 1], preferred_element_type=jnp.float32)
        level_x[level - 1] = (solved * piece_masks[level - 1]).astype(jnp.bfloat16)
    back = uplink_first * expanded[0]
    parent_full = collect_group(level_x[0], 1, place)
    update = (
        leaf_y.astype(jnp.float32) - jnp.dot(parent_full, back, preferred_element_type=jnp.float32)
    ).astype(jnp.bfloat16)
    leaf_x = leaf_term(
        lax.all_gather(update, "front", axis=1, tiled=True), matrix=upper_leaf
    ).astype(jnp.bfloat16)
    placed = jnp.concatenate([leaf_x, level_x[0], level_x[1], level_x[2]], axis=1)
    outbound = jnp.zeros_like(placed).at[:, owner_order].set(placed)
    returned = lax.all_to_all(outbound, ("leaf", "front"), split_axis=1, concat_axis=1, tiled=True)
    return jnp.zeros_like(returned).at[:, send_order].set(returned)


def solution(mesh):
    placed = (
        P(None, ("leaf", "front")),
        P(("leaf", "front")),
        P(("leaf", "front")),
        P(),
        P(None, ("leaf", "front")),
        P(None, ("leaf", "front")),
        P(None, ("leaf", "front")),
        P(None, ("leaf", "front")),
        P(None, ("leaf", "front")),
        P(None, ("leaf", "front")),
        P(None, ("leaf", "front")),
        P(None, ("leaf", "front")),
        P(None, ("leaf", "front")),
        P(None, ("leaf", "front")),
        P(None, ("leaf", "front")),
        P(None, ("leaf", "front")),
        P(None, ("leaf", "front")),
        P(None, ("leaf", "front")),
        P(None, ("leaf", "front")),
        P(None, ("leaf", "front")),
        P(None, ("leaf", "front")),
    )
    return jax.shard_map(
        per_device,
        mesh=mesh,
        in_specs=placed,
        out_specs=P(None, ("leaf", "front")),
        check_vma=False,
    )
```

profile of v0, /device:TPU:1, one launch (start us, length us, event | category | flops | bytes accessed | tf_op | source)
XLA Modules:
  0.0 459.3 jit_solution(6995919365814859507)
XLA Ops:
  9.0 2.0 gather_fusion
  12.0 11.5 %all-to-all-start = ((bf16[32,128,5]{0,2,1:T(8,128)(2,1)}), bf16[32,128,5]{0,2,1:T(8,128)(2,1)S(1)}, u32[]{:S(2)}, u32[]{:S(2)}) async-start(bf16[32,128,5]{0,2,1:T(8,128)(2,1)} %all_to_all.16), calls=%async_computation | async-start | bytes 524288 | tf_op jit(solution)/shard_map/all_to_all | solution.py:74
  25.8 3.3 bitcast_multiply_fusion.2
  30.7 3.8 all-to-all-done
  34.7 2.0 gather_fusion.1
  36.8 13.3 %all-gather = bf16[8,192,32]{1,2,0:T(8,128)(2,1)S(1)} all-gather(bf16[1,192,32]{1,2,0:T(8,128)(2,1)S(1)} %slice_bitcast_fusion), channel_id=1, replica_groups=mesh['leaf'=16,'front'=8] {'front'}, dimensions={0}, use_global_device_ids=true | all-gather | bytes 110592 | tf_op jit(solution)/shard_map/all_gather | solution.py:103
  50.6 2.0 fusion.2
  55.0 24.1 %reduce-scatter.4.cloned.1.call-done = bf16[32,512]{1,0:T(8,128)(2,1)} async-done(((bf16[32,4096]{1,0:T(8,128)(2,1)}), bf16[32,512]{1,0:T(8,128)(2,1)}) %reduce-scatter.4.cloned.1.call-update) | async-done | bytes 32784 | tf_op jit(solution)/shard_map/reduce_scatter | solution.py:120
  82.6 17.1 %all_gather.34 = bf16[32,2048]{1,0:T(8,128)(2,1)S(1)} all-gather(bf16[32,256]{1,0:T(8,128)(2,1)S(1)} %multiply_convert_fusion), channel_id=1, replica_groups=mesh['leaf'=16,'front'=8] {'front'}, dimensions={1}, use_global_device_ids=true | all-gather | bytes 147456 | tf_op jit(solution)/shard_map/all_gather | solution.py:19
  100.9 4.1 copy.74
  105.0 4.2 copy.84
  109.4 4.5 bitcast_multiply_fusion
  113.9 4.1 copy.91
  121.8 27.1 %reduce-scatter.6.cloned.1.call-done = bf16[32,512]{1,0:T(8,128)(2,1)} async-done(((bf16[32,4096]{1,0:T(8,128)(2,1)}), bf16[32,512]{1,0:T(8,128)(2,1)}) %reduce-scatter.6.cloned.1.call-update) | async-done | bytes 32784 | tf_op jit(solution)/shard_map/reduce_scatter | solution.py:120
  149.6 3.0 collective-permute-start.2
  156.4 16.6 %all_gather.35 = bf16[32,1024]{1,0:T(8,128)(2,1)S(1)} all-gather(bf16[32,128]{1,0:T(8,128)(2,1)S(1)} %multiply_convert_fusion.2), channel_id=1, replica_groups=mesh['leaf'=16,'front'=8] {'front'}, dimensions={1}, use_global_device_ids=true | all-gather | bytes 73728 | tf_op jit(solution)/shard_map/all_gather | solution.py:19
  174.3 2.2 collective-permute-done.4
  176.5 3.1 collective-permute-start.5
  181.1 2.3 copy.83
  183.6 2.7 bitcast_multiply_fusion.4
  196.3 27.5 %reduce-scatter.8.cloned.1.call-done = bf16[32,512]{1,0:T(8,128)(2,1)} async-done(((bf16[32,4096]{1,0:T(8,128)(2,1)}), bf16[32,512]{1,0:T(8,128)(2,1)}) %reduce-scatter.8.cloned.1.call-update) | async-done | bytes 32784 | tf_op jit(solution)/shard_map/reduce_scatter | solution.py:120
  227.3 2.9 collective-permute-start.7
  234.0 19.3 %all-gather.1 = bf16[8,64,32]{1,2,0:T(8,128)(2,1)S(1)} all-gather(bf16[1,64,32]{1,2,0:T(8,128)(2,1)S(1)} %fusion.79), channel_id=1, replica_groups=mesh['leaf'=16,'front'=8] {'front'}, dimensions={0}, use_global_device_ids=true | all-gather | bytes 36864 | tf_op jit(solution)/shard_map/all_gather | solution.py:19
  256.4 2.8 collective-permute-start.10
  259.2 1.9 collective-permute-done.10
  262.5 2.5 collective-permute-done.11
  266.3 16.2 %all-gather.2 = bf16[8,64,32]{1,2,0:T(8,128)(2,1)S(1)} all-gather(bf16[1,64,32]{1,2,0:T(8,128)(2,1)S(1)} %fusion.17), channel_id=1, replica_groups=mesh['leaf'=16,'front'=8] {'front'}, dimensions={0}, use_global_device_ids=true | all-gather | bytes 36864 | tf_op jit(solution)/shard_map/all_gather | solution.py:19
  285.5 2.8 collective-permute-start.13
  291.6 2.5 collective-permute-done.14
  295.5 16.2 %all-gather.3 = bf16[8,64,32]{1,2,0:T(8,128)(2,1)S(1)} all-gather(bf16[1,64,32]{1,2,0:T(8,128)(2,1)S(1)} %bitcast.122), channel_id=1, replica_groups=mesh['leaf'=16,'front'=8] {'front'}, dimensions={0}, use_global_device_ids=true | all-gather | bytes 36864 | tf_op jit(solution)/shard_map/all_gather | solution.py:19
  314.7 2.8 collective-permute-start.16
  320.8 2.5 collective-permute-done.17
  323.8 14.7 %all_gather.39 = bf16[32,1024]{1,0:T(8,128)(2,1)S(1)} all-gather(bf16[32,128]{1,0:T(8,128)(2,1)S(1)} %fusion.12), channel_id=1, replica_groups=mesh['leaf'=16,'front'=8] {'front'}, dimensions={1}, use_global_device_ids=true | all-gather | bytes 73728 | tf_op jit(solution)/shard_map/all_gather | solution.py:19
  339.6 2.4 collective-permute-done.18
  342.0 2.8 collective-permute-start.19
  344.8 2.6 collective-permute-done.19
  347.8 13.1 %all_gather.40 = bf16[32,1024]{1,0:T(8,128)(2,1)S(1)} all-gather(bf16[32,128]{1,0:T(8,128)(2,1)S(1)} %fusion.16), channel_id=1, replica_groups=mesh['leaf'=16,'front'=8] {'front'}, dimensions={1}, use_global_device_ids=true | all-gather | bytes 73728 | tf_op jit(solution)/shard_map/all_gather | solution.py:19
  362.1 2.4 collective-permute-done.20
  364.5 2.8 collective-permute-start.21
  367.2 2.6 collective-permute-done.21
  370.6 14.9 %all_gather.41 = bf16[32,2048]{1,0:T(8,128)(2,1)S(1)} all-gather(bf16[32,256]{1,0:T(8,128)(2,1)S(1)} %fusion.8), channel_id=1, replica_groups=mesh['leaf'=16,'front'=8] {'front'}, dimensions={1}, use_global_device_ids=true | all-gather | bytes 147456 | tf_op jit(solution)/shard_map/all_gather | solution.py:19
  386.7 3.8 collective-permute-done.22
  390.9 13.6 %all_gather.42 = bf16[32,2048]{1,0:T(8,128)(2,1)S(1)} all-gather(bf16[32,256]{1,0:T(8,128)(2,1)S(1)} %fusion.9), channel_id=1, replica_groups=mesh['leaf'=16,'front'=8] {'front'}, dimensions={1}, use_global_device_ids=true | all-gather | bytes 147456 | tf_op jit(solution)/shard_map/all_gather | solution.py:19
  405.7 3.8 collective-permute-done.23
  410.1 13.6 %all-gather.4 = bf16[8,192,32]{1,2,0:T(8,128)(2,1)S(1)} all-gather(bf16[1,192,32]{1,2,0:T(8,128)(2,1)S(1)} %fusion.10), channel_id=1, replica_groups=mesh['leaf'=16,'front'=8] {'front'}, dimensions={0}, use_global_device_ids=true | all-gather | bytes 110592 | tf_op jit(solution)/shard_map/all_gather | solution.py:160
  424.4 4.3 scatter_custom_fusion
  428.8 18.5 %all_to_all.24 = bf16[32,128,5]{0,2,1:T(8,128)(2,1)S(1)} all-to-all(bf16[32,128,5]{0,2,1:T(8,128)(2,1)S(1)} %all_to_all.19), channel_id=1, replica_groups=mesh['leaf'=16,'front'=8] {'leaf','front'}, dimensions={1} | all-to-all | bytes 81920 | tf_op jit(solution)/shard_map/all_to_all | solution.py:164
  447.4 4.6 %scatter_custom_fusion.1 = bf16[32,640]{0,1:T(8,128)(2,1)S(1)} fusion(s32[640]{0:T(1024)S(1)} %compare_select_fusion.1, bf16[32,640]{0,1:T(8,128)(2,1)S(1)} %reshape.88, bf16[]{:T(256)} %constant.15.clone.1), kind=kCustom, calls=%fused_computation.102 | custom fusion | bytes 204802 | tf_op jit(solution)/shard_map/scatter | solution.py:165
  (153 shorter events, 72.4 us)
Async XLA Ops:
  6.5 111.5 %copy-start = (bf16[4096,256]{1,0:T(8,128)(2,1)S(1)}, bf16[4096,256]{1,0:T(8,128)(2,1)}, u32[]{:S(2)}) copy-start(bf16[4096,256]{1,0:T(8,128)(2,1)} %param.29) | copy-start | bytes 6291460
  12.0 22.6 %all-to-all-start = ((bf16[32,128,5]{0,2,1:T(8,128)(2,1)}), bf16[32,128,5]{0,2,1:T(8,128)(2,1)S(1)}, u32[]{:S(2)}, u32[]{:S(2)}) async-start(bf16[32,128,5]{0,2,1:T(8,128)(2,1)} %all_to_all.16), calls=%async_computation | async-start | bytes 524288 | tf_op jit(solution)/shard_map/all_to_all | solution.py:74
  23.5 55.7 %reduce-scatter.4.cloned.1.call-start = ((), (), s32[]{:S(2)}) async-start(), calls=%async_computation.5 | async-start | bytes 294912 | tf_op jit(solution)/shard_map/reduce_scatter | solution.py:120
  29.1 21.2 %copy-start.6 = (bf16[1536,192]{0,1:T(8,128)(2,1)S(1)}, bf16[1536,192]{0,1:T(8,128)(2,1)}, u32[]{:S(2)}) copy-start(bf16[1536,192]{0,1:T(8,128)(2,1)} %param.27) | copy-start | bytes 1769476
  52.6 1.7 copy-start.8
  54.3 94.5 %reduce-scatter.6.cloned.1.call-start = ((), (), s32[]{:S(2)}) async-start(), calls=%async_computation.6 | async-start | bytes 294912 | tf_op jit(solution)/shard_map/reduce_scatter | solution.py:120
  79.9 2.7 collective-permute-start
  99.7 18.3 %collective-permute-start.1 = (bf16[32,2048]{1,0:T(8,128)(2,1)S(1)}, bf16[32,2048]{1,0:T(8,128)(2,1)S(1)}, u32[]{:S(2)}, u32[]{:S(2)}) collective-permute-start(bf16[32,2048]{1,0:T(8,128)(2,1)S(1)} %all_gather.34), channel_id=1, source_target_pairs={{0,8},{8,0},{16,24},{24,16},{32,40},{40,32},{48,56},{56,48},{64,72... | collective-permute-start | bytes 393224 | tf_op jit(solution)/shard_map/ppermute | solution.py:10
  105.0 4.2 copy-start.9
  118.0 1.6 copy-start.1
  121.7 102.1 %reduce-scatter.8.cloned.1.call-start = ((), (), s32[]{:S(2)}) async-start(), calls=%async_computation.7 | async-start | bytes 294912 | tf_op jit(solution)/shard_map/reduce_scatter | solution.py:120
  149.6 4.2 collective-permute-start.2
  153.8 2.6 collective-permute-start.3
  173.0 3.5 collective-permute-start.4
  176.5 11.4 %collective-permute-start.5 = (bf16[32,2048]{1,0:T(8,128)(2,1)S(1)}, bf16[32,2048]{1,0:T(8,128)(2,1)S(1)}, u32[]{:S(2)}, u32[]{:S(2)}) collective-permute-start(bf16[32,2048]{1,0:T(8,128)(2,1)S(1)} %maximum_select_fusion.18), channel_id=1, source_target_pairs={{0,16},{8,24},{16,0},{24,8},{32,48},{40,56},{48,32},{56,40},{64,80... | collective-permute-start | bytes 393224 | tf_op jit(solution)/shard_map/ppermute | solution.py:10
  179.6 3.8 copy-start.11
  224.6 2.7 collective-permute-start.6
  227.3 4.1 collective-permute-start.7
  231.4 2.5 collective-permute-start.8
  253.5 2.8 collective-permute-start.9
  256.4 4.7 %collective-permute-start.10 = (bf16[32,1024]{1,0:T(8,128)(2,1)S(1)}, bf16[32,1024]{1,0:T(8,128)(2,1)S(1)}, u32[]{:S(2)}, u32[]{:S(2)}) collective-permute-start(bf16[32,1024]{1,0:T(8,128)(2,1)S(1)} %maximum_select_fusion.24), channel_id=1, source_target_pairs={{0,16},{8,24},{16,0},{24,8},{32,48},{40,56},{48,32},{56,40},{64,80... | collective-permute-start | bytes 196616 | tf_op jit(solution)/shard_map/ppermute | solution.py:10
  261.1 62.2 %copy-start.5 = (bf16[4096,128]{0,1:T(8,128)(2,1)S(1)}, bf16[4096,128]{0,1:T(8,128)(2,1)}, u32[]{:S(2)}) copy-start(bf16[4096,128]{0,1:T(8,128)(2,1)} %get-tuple-element.10) | copy-start | bytes 3145732
  261.1 3.9 collective-permute-start.11
  282.7 2.8 collective-permute-start.12
  285.5 4.7 %collective-permute-start.13 = (bf16[32,1024]{1,0:T(8,128)(2,1)S(1)}, bf16[32,1024]{1,0:T(8,128)(2,1)S(1)}, u32[]{:S(2)}, u32[]{:S(2)}) collective-permute-start(bf16[32,1024]{1,0:T(8,128)(2,1)S(1)} %maximum_select_fusion.25), channel_id=1, source_target_pairs={{0,16},{8,24},{16,0},{24,8},{32,48},{40,56},{48,32},{56,40},{64,80... | collective-permute-start | bytes 196616 | tf_op jit(solution)/shard_map/ppermute | solution.py:10
  290.3 3.9 collective-permute-start.14
  311.8 35.6 %copy-start.10 = (bf16[4096,128]{1,0:T(8,128)(2,1)S(1)}, bf16[4096,128]{1,0:T(8,128)(2,1)}, u32[]{:S(2)}) copy-start(bf16[4096,128]{1,0:T(8,128)(2,1)} %param.33) | copy-start | bytes 3145732
  311.8 2.8 collective-permute-start.15
  314.7 55.2 %copy-start.2 = (bf16[4096,256]{0,1:T(8,128)(2,1)S(1)}, bf16[4096,256]{0,1:T(8,128)(2,1)}, u32[]{:S(2)}) copy-start(bf16[4096,256]{0,1:T(8,128)(2,1)} %get-tuple-element.8) | copy-start | bytes 6291460
  314.7 4.7 %collective-permute-start.16 = (bf16[32,1024]{1,0:T(8,128)(2,1)S(1)}, bf16[32,1024]{1,0:T(8,128)(2,1)S(1)}, u32[]{:S(2)}, u32[]{:S(2)}) collective-permute-start(bf16[32,1024]{1,0:T(8,128)(2,1)S(1)} %maximum_select_fusion.26), channel_id=1, source_target_pairs={{0,16},{8,24},{16,0},{24,8},{32,48},{40,56},{48,32},{56,40},{64,80... | collective-permute-start | bytes 196616 | tf_op jit(solution)/shard_map/ppermute | solution.py:10
  319.5 3.9 collective-permute-start.17
  338.5 3.5 collective-permute-start.18
  342.0 48.5 %copy-start.3 = (bf16[4096,256]{1,0:T(8,128)(2,1)S(1)}, bf16[4096,256]{1,0:T(8,128)(2,1)}, u32[]{:S(2)}) copy-start(bf16[4096,256]{1,0:T(8,128)(2,1)} %param.32) | copy-start | bytes 6291460
  342.0 5.4 %collective-permute-start.19 = (bf16[32,2048]{1,0:T(8,128)(2,1)S(1)}, bf16[32,2048]{1,0:T(8,128)(2,1)S(1)}, u32[]{:S(2)}, u32[]{:S(2)}) collective-permute-start(bf16[32,2048]{1,0:T(8,128)(2,1)S(1)} %maximum_select_fusion.22), channel_id=1, source_target_pairs={{0,16},{8,24},{16,0},{24,8},{32,48},{40,56},{48,32},{56,40},{64,80... | collective-permute-start | bytes 393224 | tf_op jit(solution)/shard_map/ppermute | solution.py:10
  360.9 3.5 collective-permute-start.20
  364.5 5.4 %collective-permute-start.21 = (bf16[32,2048]{1,0:T(8,128)(2,1)S(1)}, bf16[32,2048]{1,0:T(8,128)(2,1)S(1)}, u32[]{:S(2)}, u32[]{:S(2)}) collective-permute-start(bf16[32,2048]{1,0:T(8,128)(2,1)S(1)} %maximum_select_fusion.23), channel_id=1, source_target_pairs={{0,16},{8,24},{16,0},{24,8},{32,48},{40,56},{48,32},{56,40},{64,80... | collective-permute-start | bytes 393224 | tf_op jit(solution)/shard_map/ppermute | solution.py:10
  369.9 39.6 %copy-start.4 = (bf16[4096,192]{0,1:T(8,128)(2,1)S(1)}, bf16[4096,192]{0,1:T(8,128)(2,1)}, u32[]{:S(2)}) copy-start(bf16[4096,192]{0,1:T(8,128)(2,1)} %get-tuple-element.6) | copy-start | bytes 4718596
  385.6 38.3 %copy-start.7 = (bf16[1536,192]{0,1:T(8,128)(2,1)S(1)}, bf16[1536,192]{0,1:T(8,128)(2,1)}, u32[]{:S(2)}) copy-start(bf16[1536,192]{0,1:T(8,128)(2,1)} %param.28) | copy-start | bytes 1769476
  385.6 4.9 %collective-permute-start.22 = (bf16[32,2048]{1,0:T(8,128)(2,1)S(1)}, bf16[32,2048]{1,0:T(8,128)(2,1)S(1)}, u32[]{:S(2)}, u32[]{:S(2)}) collective-permute-start(bf16[32,2048]{1,0:T(8,128)(2,1)S(1)} %all_gather.41), channel_id=1, source_target_pairs={{0,8},{8,0},{16,24},{24,16},{32,40},{40,32},{48,56},{56,48},{64,72... | collective-permute-start | bytes 393224 | tf_op jit(solution)/shard_map/ppermute | solution.py:10
  404.5 4.9 %collective-permute-start.23 = (bf16[32,2048]{1,0:T(8,128)(2,1)S(1)}, bf16[32,2048]{1,0:T(8,128)(2,1)S(1)}, u32[]{:S(2)}, u32[]{:S(2)}) collective-permute-start(bf16[32,2048]{1,0:T(8,128)(2,1)S(1)} %all_gather.42), channel_id=1, source_target_pairs={{0,8},{8,0},{16,24},{24,16},{32,40},{40,32},{48,56},{56,48},{64,72... | collective-permute-start | bytes 393224 | tf_op jit(solution)/shard_map/ppermute | solution.py:10
Sparse Core Ops, SparseCore 0:
  54.4 24.6 reduce-scatter.3
  121.8 26.9 reduce-scatter.5
  196.4 27.3 reduce-scatter.7
where the time goes:
time: 461 us; the launch traced here: 459 us
  blocking collectives  187 us (41%)
  waiting for transfers between devices  126 us (27%)
  starting transfers between devices  55 us (12%)
  local copies, waits for them, and re-layouts  43.1 us (9%)
  other arithmetic  23.3 us (5%)
  between operations  13.6 us (3%)
  matrix products  11.4 us (2%)
    all_gather x9, blocking collectives, collect_group(): gathered = lax.all_gather(portion, 'front', axis=1, tiled=True)  142 us
    reduce_scatter x3, waiting for transfers between devices, per_device(): lax.psum_scatter(term.astype(jnp.bfloat16), 'front', scatter_dimension=1,...  78.7 us
    ppermute x24, starting transfers between devices, partner_2(): return lax.ppermute(value, axis, pairs)  43.4 us
    ppermute x24, waiting for transfers between devices, partner_2(): return lax.ppermute(value, axis, pairs)  43.3 us
    all_to_all x1, blocking collectives, per_device(): lax.all_to_all(outbound, ('leaf', 'front'), split_axis=1, concat_axis=1,...  18.5 us
    unnamed x36, local copies, waits for them, and re-layouts  16.5 us
    all_gather x1, blocking collectives, per_device(): lax.all_gather(update, 'front', axis=1, tiled=True)  13.6 us
    all_gather x1, blocking collectives, per_device(): lax.all_gather(leaf_rhs, 'front', axis=1, tiled=True)  13.3 us
  transfers between devices with their start and end apart: 28, of which 26 were waited for; matrix products, arithmetic and copies ran while one was open for 8% of the time, Pallas kernels for 0%

commit v1 on v0

--- a/solution.py
+++ b/solution.py
@@ -16,7 +16,9 @@
 
 
 def collect_group(portion, level, place):
-    gathered = lax.all_gather(portion, "front", axis=1, tiled=True)
+    gathered = jnp.concatenate(
+        lax.all_to_all(jnp.stack([portion] * lax.axis_size("front")), "front", 0, 0), axis=1
+    )
     for level_bit in range(level):
         partner = partner_2(gathered, "leaf", level_bit)
         upper_side = place >> level_bit & 1 == 1

time: 461 us -> 422 us (0.915)
  blocking collectives: 187 us -> 150 us
    all_gather x9 -> x0, blocking collectives: 142 us -> none  [collect_group(): gathered = lax.all_gather(portion, 'front', axis=1, tiled=True)]
    all_to_all x0 -> x9, blocking collectives: none -> 104 us  [collect_group(): lax.all_to_all(jnp.stack([portion] * lax.axis_size('front')), 'front', 0, 0)]
    unnamed x36 -> x39, local copies, waits for them, and re-layouts: 16.5 us -> 16.8 us
where the time goes in v1:
time: 422 us; the launch traced here: 421 us
  blocking collectives  150 us (36%)
  waiting for transfers between devices  124 us (29%)
  starting transfers between devices  54.4 us (13%)
  local copies, waits for them, and re-layouts  44 us (10%)
  other arithmetic  23.3 us (6%)
  between operations  13.7 us (3%)
  matrix products  11.5 us (3%)
    all_to_all x9, blocking collectives, collect_group(): lax.all_to_all(jnp.stack([portion] * lax.axis_size('front')), 'front', 0, 0)  104 us
    reduce_scatter x3, waiting for transfers between devices, per_device(): lax.psum_scatter(term.astype(jnp.bfloat16), 'front', scatter_dimension=1,...  78.9 us
    ppermute x24, starting transfers between devices, partner_2(): return lax.ppermute(value, axis, pairs)  42.7 us
    ppermute x24, waiting for transfers between devices, partner_2(): return lax.ppermute(value, axis, pairs)  41.2 us
    all_to_all x1, blocking collectives, per_device(): lax.all_to_all(outbound, ('leaf', 'front'), split_axis=1, concat_axis=1,...  18.5 us
    unnamed x39, local copies, waits for them, and re-layouts  16.8 us
    all_gather x1, blocking collectives, per_device(): lax.all_gather(update, 'front', axis=1, tiled=True)  14.6 us
    all_gather x1, blocking collectives, per_device(): lax.all_gather(leaf_rhs, 'front', axis=1, tiled=True)  13.3 us
  transfers between devices with their start and end apart: 28, of which 26 were waited for; matrix products, arithmetic and copies ran while one was open for 8% of the time, Pallas kernels for 0%

profile of v1, /device:TPU:1, one launch (start us, length us, event | category | flops | bytes accessed | tf_op | source)
XLA Modules:
  0.0 420.9 jit_solution(3300213880173162304)
XLA Ops:
  9.0 2.0 gather_fusion
  12.0 11.5 %all-to-all-start = ((bf16[32,128,5]{0,2,1:T(8,128)(2,1)}), bf16[32,128,5]{0,2,1:T(8,128)(2,1)S(1)}, u32[]{:S(2)}, u32[]{:S(2)}) async-start(bf16[32,128,5]{0,2,1:T(8,128)(2,1)} %all_to_all.43), calls=%async_computation | async-start | bytes 524288 | tf_op jit(solution)/shard_map/all_to_all | solution.py:76
  25.8 3.3 bitcast_multiply_fusion.2
  30.7 3.8 all-to-all-done
  36.8 13.3 %all-gather = bf16[8,192,32]{1,2,0:T(8,128)(2,1)S(1)} all-gather(bf16[1,192,32]{1,2,0:T(8,128)(2,1)S(1)} %slice_bitcast_fusion), channel_id=1, replica_groups=mesh['leaf'=16,'front'=8] {'front'}, dimensions={0}, use_global_device_ids=true | all-gather | bytes 110592 | tf_op jit(solution)/shard_map/all_gather | solution.py:105
  50.6 2.0 fusion.2
  55.0 24.1 %reduce-scatter.4.cloned.1.call-done = bf16[32,512]{1,0:T(8,128)(2,1)} async-done(((bf16[32,4096]{1,0:T(8,128)(2,1)}), bf16[32,512]{1,0:T(8,128)(2,1)}) %reduce-scatter.4.cloned.1.call-update) | async-done | bytes 32784 | tf_op jit(solution)/shard_map/reduce_scatter | solution.py:122
  82.6 12.1 %all_to_all.69 = bf16[8,32,256]{2,1,0:T(8,128)(2,1)S(1)} all-to-all(bf16[8,32,256]{2,1,0:T(8,128)(2,1)S(1)} %stack.18), channel_id=1, replica_groups=mesh['leaf'=16,'front'=8] {'front'}, dimensions={0} | all-to-all | bytes 262144 | tf_op jit(solution)/shard_map/all_to_all | solution.py:20
  96.0 4.1 copy.85
  100.2 4.2 copy.98
  104.6 4.5 %bitcast_multiply_fusion = (bf16[4096,256]{0,1:T(8,128)(2,1)}, bf16[4096,256]{0,1:T(8,128)(2,1)}) fusion(bf16[4096,256]{0,1:T(8,128)(2,1)} %copy.98, bf16[4096,4]{0,1:T(4,128)(2,1)S(1)} %convert_element_type.183, bf16[4096,256]{0,1:T(8,128)(2,1)} %copy.85), kind=kLoop, calls=%fused_computation.4 | loop fusion | flops 2097152 | bytes 8421376 | tf_op jit(solution)/shard_map/mul | solution.py:147
  109.1 4.1 copy.107
  116.9 27.5 %reduce-scatter.6.cloned.1.call-done = bf16[32,512]{1,0:T(8,128)(2,1)} async-done(((bf16[32,4096]{1,0:T(8,128)(2,1)}), bf16[32,512]{1,0:T(8,128)(2,1)}) %reduce-scatter.6.cloned.1.call-update) | async-done | bytes 32784 | tf_op jit(solution)/shard_map/reduce_scatter | solution.py:122
  145.2 2.9 collective-permute-start.2
  152.0 12.8 %all_to_all.70 = bf16[8,32,128]{2,1,0:T(8,128)(2,1)S(1)} all-to-all(bf16[8,32,128]{2,1,0:T(8,128)(2,1)S(1)} %stack.19), channel_id=1, replica_groups=mesh['leaf'=16,'front'=8] {'front'}, dimensions={0} | all-to-all | bytes 131072 | tf_op jit(solution)/shard_map/all_to_all | solution.py:20
  168.0 3.0 collective-permute-start.5
  172.5 2.3 copy.95
  175.0 2.7 bitcast_multiply_fusion.4
  187.8 27.3 %reduce-scatter.8.cloned.1.call-done = bf16[32,512]{1,0:T(8,128)(2,1)} async-done(((bf16[32,4096]{1,0:T(8,128)(2,1)}), bf16[32,512]{1,0:T(8,128)(2,1)}) %reduce-scatter.8.cloned.1.call-update) | async-done | bytes 32784 | tf_op jit(solution)/shard_map/reduce_scatter | solution.py:122
  218.5 2.9 collective-permute-start.7
  225.4 13.9 %all_to_all.71 = bf16[8,2,1024]{2,1,0:T(2,128)(2,1)S(1)} all-to-all(bf16[8,2,1024]{2,1,0:T(2,128)(2,1)S(1)} %reshape.204), channel_id=1, replica_groups=mesh['leaf'=16,'front'=8] {'front'}, dimensions={0} | all-to-all | bytes 65536 | tf_op jit(solution)/shard_map/all_to_all | solution.py:20
  242.5 2.7 collective-permute-start.10
  245.2 2.0 collective-permute-done.10
  248.6 2.6 collective-permute-done.11
  252.6 11.3 %all_to_all.72 = bf16[8,2,1024]{2,1,0:T(2,128)(2,1)S(1)} all-to-all(bf16[8,2,1024]{2,1,0:T(2,128)(2,1)S(1)} %reshape.206), channel_id=1, replica_groups=mesh['leaf'=16,'front'=8] {'front'}, dimensions={0} | all-to-all | bytes 65536 | tf_op jit(solution)/shard_map/all_to_all | solution.py:20
  267.0 2.7 collective-permute-start.13
  269.7 2.0 collective-permute-done.13
  273.0 2.6 collective-permute-done.14
  277.0 11.3 %all_to_all.73 = bf16[8,2,1024]{2,1,0:T(2,128)(2,1)S(1)} all-to-all(bf16[8,2,1024]{2,1,0:T(2,128)(2,1)S(1)} %reshape.208), channel_id=1, replica_groups=mesh['leaf'=16,'front'=8] {'front'}, dimensions={0} | all-to-all | bytes 65536 | tf_op jit(solution)/shard_map/all_to_all | solution.py:20
  291.4 2.7 collective-permute-start.16
  294.2 2.0 collective-permute-done.16
  297.5 2.6 collective-permute-done.17
  300.6 11.5 %all_to_all.74 = bf16[8,32,128]{2,1,0:T(8,128)(2,1)S(1)} all-to-all(bf16[8,32,128]{2,1,0:T(8,128)(2,1)S(1)} %stack.23), channel_id=1, replica_groups=mesh['leaf'=16,'front'=8] {'front'}, dimensions={0} | all-to-all | bytes 131072 | tf_op jit(solution)/shard_map/all_to_all | solution.py:20
  313.2 2.0 collective-permute-done.18
  315.3 2.7 collective-permute-start.19
  318.0 2.7 collective-permute-done.19
  321.0 10.4 %all_to_all.75 = bf16[8,32,128]{2,1,0:T(8,128)(2,1)S(1)} all-to-all(bf16[8,32,128]{2,1,0:T(8,128)(2,1)S(1)} %stack.24), channel_id=1, replica_groups=mesh['leaf'=16,'front'=8] {'front'}, dimensions={0} | all-to-all | bytes 131072 | tf_op jit(solution)/shard_map/all_to_all | solution.py:20
  332.6 2.0 collective-permute-done.20
  334.6 2.7 collective-permute-start.21
  337.3 2.7 collective-permute-done.21
  340.8 10.9 %all_to_all.76 = bf16[8,32,256]{2,1,0:T(8,128)(2,1)S(1)} all-to-all(bf16[8,32,256]{2,1,0:T(8,128)(2,1)S(1)} %stack.25), channel_id=1, replica_groups=mesh['leaf'=16,'front'=8] {'front'}, dimensions={0} | all-to-all | bytes 262144 | tf_op jit(solution)/shard_map/all_to_all | solution.py:20
  352.8 3.0 collective-permute-done.22
  356.3 9.6 %all_to_all.77 = bf16[8,32,256]{2,1,0:T(8,128)(2,1)S(1)} all-to-all(bf16[8,32,256]{2,1,0:T(8,128)(2,1)S(1)} %stack.26), channel_id=1, replica_groups=mesh['leaf'=16,'front'=8] {'front'}, dimensions={0} | all-to-all | bytes 262144 | tf_op jit(solution)/shard_map/all_to_all | solution.py:20
  367.1 3.0 collective-permute-done.23
  370.7 14.6 %all-gather.1 = bf16[8,192,32]{1,2,0:T(8,128)(2,1)S(1)} all-gather(bf16[1,192,32]{1,2,0:T(8,128)(2,1)S(1)} %fusion.10), channel_id=1, replica_groups=mesh['leaf'=16,'front'=8] {'front'}, dimensions={0}, use_global_device_ids=true | all-gather | bytes 110592 | tf_op jit(solution)/shard_map/all_gather | solution.py:162
  386.1 4.3 %scatter_custom_fusion = bf16[32,640]{0,1:T(8,128)(2,1)S(1)} fusion(s32[640]{0:T(1024)S(1)} %compare_select_fusion, bf16[640,32]{1,0:T(8,128)(2,1)S(1)} %copy.102, bf16[]{:T(256)} %constant.15.clone.1), kind=kCustom, calls=%fused_computation.111 | custom fusion | bytes 40962 | tf_op jit(solution)/shard_map/scatter | solution.py:165
  390.4 18.5 %all_to_all.78 = bf16[32,128,5]{0,2,1:T(8,128)(2,1)S(1)} all-to-all(bf16[32,128,5]{0,2,1:T(8,128)(2,1)S(1)} %all_to_all.55), channel_id=1, replica_groups=mesh['leaf'=16,'front'=8] {'leaf','front'}, dimensions={1} | all-to-all | bytes 81920 | tf_op jit(solution)/shard_map/all_to_all | solution.py:166
  409.0 4.6 %scatter_custom_fusion.1 = bf16[32,640]{0,1:T(8,128)(2,1)S(1)} fusion(s32[640]{0:T(1024)S(1)} %compare_select_fusion.1, bf16[32,640]{0,1:T(8,128)(2,1)S(1)} %reshape.178, bf16[]{:T(256)} %constant.15.clone.1), kind=kCustom, calls=%fused_computation.101 | custom fusion | bytes 204802 | tf_op jit(solution)/shard_map/scatter | solution.py:167
  (174 shorter events, 73.3 us)
Async XLA Ops:
  6.5 106.6 %copy-start = (bf16[4096,256]{1,0:T(8,128)(2,1)S(1)}, bf16[4096,256]{1,0:T(8,128)(2,1)}, u32[]{:S(2)}) copy-start(bf16[4096,256]{1,0:T(8,128)(2,1)} %param.29) | copy-start | bytes 6291460
  12.0 22.6 %all-to-all-start = ((bf16[32,128,5]{0,2,1:T(8,128)(2,1)}), bf16[32,128,5]{0,2,1:T(8,128)(2,1)S(1)}, u32[]{:S(2)}, u32[]{:S(2)}) async-start(bf16[32,128,5]{0,2,1:T(8,128)(2,1)} %all_to_all.43), calls=%async_computation | async-start | bytes 524288 | tf_op jit(solution)/shard_map/all_to_all | solution.py:76
  23.5 55.7 %reduce-scatter.4.cloned.1.call-start = ((), (), s32[]{:S(2)}) async-start(), calls=%async_computation.14 | async-start | bytes 294912 | tf_op jit(solution)/shard_map/reduce_scatter | solution.py:122
  29.1 21.2 %copy-start.6 = (bf16[1536,192]{0,1:T(8,128)(2,1)S(1)}, bf16[1536,192]{0,1:T(8,128)(2,1)}, u32[]{:S(2)}) copy-start(bf16[1536,192]{0,1:T(8,128)(2,1)} %param.27) | copy-start | bytes 1769476
  52.6 1.7 copy-start.8
  54.3 90.1 %reduce-scatter.6.cloned.1.call-start = ((), (), s32[]{:S(2)}) async-start(), calls=%async_computation.15 | async-start | bytes 294912 | tf_op jit(solution)/shard_map/reduce_scatter | solution.py:122
  79.9 2.7 collective-permute-start
  94.8 18.4 %collective-permute-start.1 = (bf16[32,2048]{1,0:T(8,128)(2,1)S(1)}, bf16[32,2048]{1,0:T(8,128)(2,1)S(1)}, u32[]{:S(2)}, u32[]{:S(2)}) collective-permute-start(bf16[32,2048]{1,0:T(8,128)(2,1)S(1)} %bitcast.126), channel_id=1, source_target_pairs={{0,8},{8,0},{16,24},{24,16},{32,40},{40,32},{48,56},{56,48},{64,72... | collective-permute-start | bytes 393224 | tf_op jit(solution)/shard_map/ppermute | solution.py:10
  100.2 4.2 copy-start.9
  113.1 1.6 copy-start.1
  116.9 98.2 %reduce-scatter.8.cloned.1.call-start = ((), (), s32[]{:S(2)}) async-start(), calls=%async_computation.16 | async-start | bytes 294912 | tf_op jit(solution)/shard_map/reduce_scatter | solution.py:122
  145.2 4.2 collective-permute-start.2
  149.4 2.6 collective-permute-start.3
  164.8 3.1 collective-permute-start.4
  168.0 11.3 %collective-permute-start.5 = (bf16[32,2048]{1,0:T(8,128)(2,1)S(1)}, bf16[32,2048]{1,0:T(8,128)(2,1)}, u32[]{:S(2)}, u32[]{:S(2)}) collective-permute-start(bf16[32,2048]{1,0:T(8,128)(2,1)S(1)} %maximum_select_fusion.18), channel_id=1, source_target_pairs={{0,16},{8,24},{16,0},{24,8},{32,48},{40,56},{48,32},{56,40},{64,80... | collective-permute-start | bytes 393224 | tf_op jit(solution)/shard_map/ppermute | solution.py:10
  171.0 3.8 copy-start.11
  215.8 2.7 collective-permute-start.6
  218.5 4.1 collective-permute-start.7
  222.7 2.5 collective-permute-start.8
  239.6 2.8 collective-permute-start.9
  242.5 4.7 %collective-permute-start.10 = (bf16[32,1024]{1,0:T(8,128)(2,1)S(1)}, bf16[32,1024]{1,0:T(8,128)(2,1)S(1)}, u32[]{:S(2)}, u32[]{:S(2)}) collective-permute-start(bf16[32,1024]{1,0:T(8,128)(2,1)S(1)} %maximum_select_fusion.24), channel_id=1, source_target_pairs={{0,16},{8,24},{16,0},{24,8},{32,48},{40,56},{48,32},{56,40},{64,80... | collective-permute-start | bytes 196616 | tf_op jit(solution)/shard_map/ppermute | solution.py:10
  247.2 52.9 %copy-start.5 = (bf16[4096,128]{0,1:T(8,128)(2,1)S(1)}, bf16[4096,128]{0,1:T(8,128)(2,1)}, u32[]{:S(2)}) copy-start(bf16[4096,128]{0,1:T(8,128)(2,1)} %get-tuple-element.10) | copy-start | bytes 3145732
  247.2 3.9 collective-permute-start.11
  264.1 2.8 collective-permute-start.12
  267.0 4.7 %collective-permute-start.13 = (bf16[32,1024]{1,0:T(8,128)(2,1)S(1)}, bf16[32,1024]{1,0:T(8,128)(2,1)S(1)}, u32[]{:S(2)}, u32[]{:S(2)}) collective-permute-start(bf16[32,1024]{1,0:T(8,128)(2,1)S(1)} %maximum_select_fusion.25), channel_id=1, source_target_pairs={{0,16},{8,24},{16,0},{24,8},{32,48},{40,56},{48,32},{56,40},{64,80... | collective-permute-start | bytes 196616 | tf_op jit(solution)/shard_map/ppermute | solution.py:10
  271.7 3.9 collective-permute-start.14
  288.6 32.1 %copy-start.10 = (bf16[4096,128]{1,0:T(8,128)(2,1)S(1)}, bf16[4096,128]{1,0:T(8,128)(2,1)}, u32[]{:S(2)}) copy-start(bf16[4096,128]{1,0:T(8,128)(2,1)} %param.33) | copy-start | bytes 3145732
  288.6 2.8 collective-permute-start.15
  291.4 4.7 %collective-permute-start.16 = (bf16[32,1024]{1,0:T(8,128)(2,1)S(1)}, bf16[32,1024]{1,0:T(8,128)(2,1)S(1)}, u32[]{:S(2)}, u32[]{:S(2)}) collective-permute-start(bf16[32,1024]{1,0:T(8,128)(2,1)S(1)} %maximum_select_fusion.26), channel_id=1, source_target_pairs={{0,16},{8,24},{16,0},{24,8},{32,48},{40,56},{48,32},{56,40},{64,80... | collective-permute-start | bytes 196616 | tf_op jit(solution)/shard_map/ppermute | solution.py:10
  296.2 3.9 collective-permute-start.17
  300.1 39.9 %copy-start.2 = (bf16[4096,256]{0,1:T(8,128)(2,1)S(1)}, bf16[4096,256]{0,1:T(8,128)(2,1)}, u32[]{:S(2)}) copy-start(bf16[4096,256]{0,1:T(8,128)(2,1)} %get-tuple-element.8) | copy-start | bytes 6291460
  312.1 3.1 collective-permute-start.18
  315.3 5.4 %collective-permute-start.19 = (bf16[32,2048]{1,0:T(8,128)(2,1)S(1)}, bf16[32,2048]{1,0:T(8,128)(2,1)S(1)}, u32[]{:S(2)}, u32[]{:S(2)}) collective-permute-start(bf16[32,2048]{1,0:T(8,128)(2,1)S(1)} %maximum_select_fusion.22), channel_id=1, source_target_pairs={{0,16},{8,24},{16,0},{24,8},{32,48},{40,56},{48,32},{56,40},{64,80... | collective-permute-start | bytes 393224 | tf_op jit(solution)/shard_map/ppermute | solution.py:10
  321.0 34.9 %copy-start.3 = (bf16[4096,256]{1,0:T(8,128)(2,1)S(1)}, bf16[4096,256]{1,0:T(8,128)(2,1)}, u32[]{:S(2)}) copy-start(bf16[4096,256]{1,0:T(8,128)(2,1)} %param.32) | copy-start | bytes 6291460
  331.4 3.1 collective-permute-start.20
  334.6 5.4 %collective-permute-start.21 = (bf16[32,2048]{1,0:T(8,128)(2,1)S(1)}, bf16[32,2048]{1,0:T(8,128)(2,1)S(1)}, u32[]{:S(2)}, u32[]{:S(2)}) collective-permute-start(bf16[32,2048]{1,0:T(8,128)(2,1)S(1)} %maximum_select_fusion.23), channel_id=1, source_target_pairs={{0,16},{8,24},{16,0},{24,8},{32,48},{40,56},{48,32},{56,40},{64,80... | collective-permute-start | bytes 393224 | tf_op jit(solution)/shard_map/ppermute | solution.py:10
  340.7 29.4 %copy-start.4 = (bf16[4096,192]{0,1:T(8,128)(2,1)S(1)}, bf16[4096,192]{0,1:T(8,128)(2,1)}, u32[]{:S(2)}) copy-start(bf16[4096,192]{0,1:T(8,128)(2,1)} %get-tuple-element.6) | copy-start | bytes 4718596
  351.6 4.2 %collective-permute-start.22 = (bf16[32,2048]{1,0:T(8,128)(2,1)S(1)}, bf16[32,2048]{1,0:T(8,128)(2,1)S(1)}, u32[]{:S(2)}, u32[]{:S(2)}) collective-permute-start(bf16[32,2048]{1,0:T(8,128)(2,1)S(1)} %bitcast.128), channel_id=1, source_target_pairs={{0,8},{8,0},{16,24},{24,16},{32,40},{40,32},{48,56},{56,48},{64,72... | collective-permute-start | bytes 393224 | tf_op jit(solution)/shard_map/ppermute | solution.py:10
  356.3 29.2 %copy-start.7 = (bf16[1536,192]{0,1:T(8,128)(2,1)S(1)}, bf16[1536,192]{0,1:T(8,128)(2,1)}, u32[]{:S(2)}) copy-start(bf16[1536,192]{0,1:T(8,128)(2,1)} %param.28) | copy-start | bytes 1769476
  365.9 4.2 %collective-permute-start.23 = (bf16[32,2048]{1,0:T(8,128)(2,1)S(1)}, bf16[32,2048]{1,0:T(8,128)(2,1)S(1)}, u32[]{:S(2)}, u32[]{:S(2)}) collective-permute-start(bf16[32,2048]{1,0:T(8,128)(2,1)S(1)} %bitcast.136), channel_id=1, source_target_pairs={{0,8},{8,0},{16,24},{24,16},{32,40},{40,32},{48,56},{56,48},{64,72... | collective-permute-start | bytes 393224 | tf_op jit(solution)/shard_map/ppermute | solution.py:10
Sparse Core Ops, SparseCore 0:
  54.4 24.6 reduce-scatter.3
  117.0 27.3 reduce-scatter.5
  187.9 27.1 reduce-scatter.7
